TPU v7x, 32 devices: a whole 2x2x4 slice. The times are simulated.
32 devices in a mesh: grp: 2 (over x), occ: 16 (over z, y, core).
Axes of the slice: x: 2, y: 2, z: 4, core: 2. Of those that a mesh axis runs over, the one named last changes fastest.
Arguments:
- orbital_blocks: bfloat16 [32, 512, 4096], P(('grp', 'occ')), parts along dimension 0, may hold values from -0.75 to 0.75
- eps_occ: float32 [32], P('grp'), parts along dimension 0, may hold values from -2 to -0.5
- eps_vir: float32 [1024], P('grp'), parts along dimension 0, may hold values from 0.2 to 3
- pair_mask: int32 [32, 2], P('grp'), parts along dimension 0, may hold values 0 or 1
Outputs:
- grad_density: float32 [32, 512, 4096], P(('grp', 'occ')), parts along dimension 0
There are 2 independent parts, one for each index of `grp`. A program takes and returns all parts, laid end to end along the dimension named above; each array names one. Nothing has to cross between parts.
Inputs may be any that keep to these rules, and one draw needn't show every extreme that they name: pair_mask[i, 0] selects the pair (i, i + 1) and pair_mask[i, 1] the pair (i, i + 8); entries of pairs that do not exist are unused.
All inputs are finite; a program needn't handle non-finite values.
Results may differ from a plain program's by a relative error of at most 0.0026.
Values may be sent and summed in bfloat16 or wider, within the bound.
A program may use at most 128 MiB of HBM per device.

v0:
```python
import jax
import jax.numpy as jnp
from jax import lax
from jax.sharding import PartitionSpec as P


def padded_2(cells, sides, width):
    for axis, dim in sides:
        count = lax.axis_size(axis)
        ends = count - 1
        head = lax.slice_in_dim(cells, 0, width, axis=dim)
        tail = lax.slice_in_dim(cells, cells.shape[dim] - width, cells.shape[dim], axis=dim)
        cells = jnp.concatenate(
            [
                lax.ppermute(tail, axis, [(i, (i + 1) % count) for i in range(ends)]),
                cells,
                lax.ppermute(head, axis, [((i + 1) % count, i) for i in range(ends)]),
            ],
            axis=dim,
        )
    return cells


def passed_along(shard, axis, by):
    peers = lax.axis_size(axis)
    return lax.ppermute(shard, axis, [(i, (i + by) % peers) for i in range(peers)])


def amplitudes(home_block, partner_block, home_energy, partner_energy, eps_vir, keep_pair):
    integrals = jnp.einsum(
        "rap,rbp->rab", home_block, partner_block, preferred_element_type=jnp.float32
    )
    denominator = (
        eps_vir[None, :, None]
        + eps_vir[None, None, :]
        - (home_energy + partner_energy)[:, None, None]
    )
    single = -integrals / denominator
    doubled = 2.0 * single - jnp.swapaxes(single, 1, 2)
    return jnp.where(keep_pair[:, None, None], doubled, 0.0).astype(jnp.bfloat16)


def apply_left(weights, blocks):
    return jnp.einsum("rab,rbp->rap", weights, blocks, preferred_element_type=jnp.float32)


def rows_at(table, start, slots):
    return lax.dynamic_slice_in_dim(table, start, slots, 0)


def local(orbital_blocks, eps_occ, eps_vir, pair_mask):
    slots = orbital_blocks.shape[0]
    cycle_size = lax.axis_size("occ")
    half_cycle = cycle_size // 2
    position = lax.axis_index("occ")
    home_energy = rows_at(eps_occ, position * slots, slots)
    home_mask = rows_at(pair_mask, position * slots, slots)
    padded = padded_2(orbital_blocks, (("occ", 0),), slots)
    lower_block = padded[:slots]
    upper_block = padded[2 * slots :]
    across_block = passed_along(orbital_blocks, "occ", half_cycle)
    partner_position = (position + half_cycle) % cycle_size
    lower_mask = rows_at(pair_mask, (position - 1) * slots, slots)
    across_mask = rows_at(pair_mask, jnp.minimum(position, partner_position) * slots, slots)
    upper_keep = (position < cycle_size - 1) & (home_mask[:, 0] == 1)
    lower_keep = (position > 0) & (lower_mask[:, 0] == 1)
    across_keep = across_mask[:, 1] == 1
    upper_weights = amplitudes(
        orbital_blocks,
        upper_block,
        home_energy,
        rows_at(eps_occ, (position + 1) * slots, slots),
        eps_vir,
        upper_keep,
    )
    lower_weights = amplitudes(
        orbital_blocks,
        lower_block,
        home_energy,
        rows_at(eps_occ, (position - 1) * slots, slots),
        eps_vir,
        lower_keep,
    )
    across_weights = amplitudes(
        orbital_blocks,
        across_block,
        home_energy,
        rows_at(eps_occ, partner_position * slots, slots),
        eps_vir,
        across_keep,
    )
    gradient = apply_left(upper_weights, upper_block) + apply_left(lower_weights, lower_block)
    gradient = gradient + apply_left(across_weights, across_block)
    return gradient


def solution(mesh):
    in_specs = (P(("grp", "occ"), None, None), P("grp"), P("grp"), P("grp", None))
    out_specs = P(("grp", "occ"), None, None)
    return jax.shard_map(local, mesh=mesh, in_specs=in_specs, out_specs=out_specs, check_vma=False)
```

profile of v0, /device:TPU:0, one launch (start us, length us, event | category | flops | bytes accessed | tf_op | source)
XLA Modules:
  0.0 262.9 jit_solution(18062691794603014838)
XLA Ops:
  0.0 0.0 copy-start.3
  0.0 4.5 %collective-permute-start.1 = (bf16[1,512,4096]{2,1,0:T(8,128)(2,1)}, bf16[1,512,4096]{2,1,0:T(8,128)(2,1)}, u32[]{:S(2)}, u32[]{:S(2)}) collective-permute-start(bf16[1,512,4096]{2,1,0:T(8,128)(2,1)} %param.4), channel_id=1, source_target_pairs={{0,1},{1,2},{2,3},{3,4},{4,5},{5,6},{6,7},{7,8},{8,9},{9,10},{10,1... | collective-permute-start | bytes 12582920 | tf_op jit(solution)/shard_map/ppermute | solution.py:15
  4.5 1.3 collective-permute-start
  5.8 4.9 %collective-permute-start.2 = (bf16[1,512,4096]{2,1,0:T(8,128)(2,1)}, bf16[1,512,4096]{2,1,0:T(8,128)(2,1)}, u32[]{:S(2)}, u32[]{:S(2)}) collective-permute-start(bf16[1,512,4096]{2,1,0:T(8,128)(2,1)} %param.4), channel_id=1, source_target_pairs={{0,8},{1,9},{2,10},{3,11},{4,12},{5,13},{6,14},{7,15},{8,0},{9,1},... | collective-permute-start | bytes 12582920 | tf_op jit(solution)/shard_map/ppermute | solution.py:26
  10.7 0.9 constant_dynamic-slice_fusion
  11.6 0.5 slice.10
  12.1 1.5 fusion.70
  17.4 1.0 add_subtract_fusion
  18.4 0.3 copy.5
  18.7 0.5 slice.9
  20.5 0.3 copy.10
  20.8 0.5 slice.11
  22.0 0.0 collective-permute-done.1
  22.0 0.0 copy-done.3
  22.0 5.8 %fusion.37 = f32[512,512]{0,1:T(8,128)S(1)} fusion(bf16[1,512,4096]{2,1,0:T(8,128)(2,1)} %collective-permute-done.1, bf16[1,512,4096]{2,1,0:T(8,128)(2,1)} %param.4, f32[]{:T(128)} %bitcast.14, f32[512]{0:T(512)S(1)} %copy-done.3), kind=kOutput, calls=%fused_computation.23 | convolution fusion | flops 2148532224 | bytes 9439236 | tf_op jit(solution)/shard_map/rap,rbp->rab/dot_general | solution.py:30
  27.9 1.3 copy.8
  29.2 0.0 collective-permute-done
  29.2 5.8 %fusion.42 = f32[512,512]{1,0:T(8,128)S(1)} fusion(f32[512,512]{1,0:T(8,128)S(1)} %copy.5, bf16[1,512,4096]{2,1,0:T(8,128)(2,1)} %collective-permute-done, bf16[1,512,4096]{2,1,0:T(8,128)(2,1)} %param.4), kind=kOutput, calls=%fused_computation.24 | convolution fusion | flops 2148007936 | bytes 10485760 | tf_op jit(solution)/shard_map/rap,rbp->rab/dot_general | solution.py:30
  35.0 0.0 copy-start
  35.0 1.0 copy-done
  36.1 0.1 multiply_bitcast_fusion.1
  36.2 1.3 copy.6
  37.5 198.2 %collective-permute-done.2 = bf16[1,512,4096]{2,1,0:T(8,128)(2,1)} collective-permute-done((bf16[1,512,4096]{2,1,0:T(8,128)(2,1)}, bf16[1,512,4096]{2,1,0:T(8,128)(2,1)}, u32[]{:S(2)}, u32[]{:S(2)}) %collective-permute-start.2) | collective-permute-done | bytes 4194336 | tf_op jit(solution)/shard_map/ppermute | solution.py:26
  235.7 5.8 %fusion.32 = f32[512,512]{1,0:T(8,128)S(1)} fusion(f32[512,512]{1,0:T(8,128)S(1)} %copy.10, bf16[1,512,4096]{2,1,0:T(8,128)(2,1)} %collective-permute-done.2, bf16[1,512,4096]{2,1,0:T(8,128)(2,1)} %param.4), kind=kOutput, calls=%fused_computation.22 | convolution fusion | flops 2148007936 | bytes 10485760 | tf_op jit(solution)/shard_map/rap,rbp->rab/dot_general | solution.py:30
  241.5 1.1 multiply_bitcast_fusion
  242.6 1.6 copy.11
  244.1 0.0 copy-start.1
  244.2 0.0 copy-start.2
  244.2 5.0 %fusion.6 = f32[512,4096]{1,0:T(8,128)S(1)} fusion(bf16[1,512,4096]{2,1,0:T(8,128)(2,1)} %collective-permute-done.1, f32[512,512]{0,1:T(8,128)S(1)} %fusion.37, f32[512,512]{1,0:T(8,128)} %copy.8, pred[]{:T(512)} %bitcast.12), kind=kOutput, calls=%fused_computation.5 | convolution fusion | flops 2148532224 | bytes 14680065 | tf_op jit(solution)/shard_map/rab,rbp->rap/dot_general | solution.py:44
  249.2 0.0 copy-done.1
  249.2 0.0 copy-done.2
  249.2 5.0 %fusion.10 = f32[512,4096]{1,0:T(8,128)S(1)} fusion(bf16[1,512,4096]{2,1,0:T(8,128)(2,1)} %collective-permute-done, f32[1,512,512]{1,2,0:T(8,128)S(1)} %copy-done.2, f32[512,512]{1,0:T(8,128)S(1)} %copy-done.1, pred[]{:T(512)} %bitcast.2), kind=kOutput, calls=%fused_computation.9 | convolution fusion | flops 2148270080 | bytes 14680065 | tf_op jit(solution)/shard_map/rab,rbp->rap/dot_general | solution.py:44
  254.2 8.7 %add_bitcast_fusion = f32[1,512,4096]{2,1,0:T(8,128)} fusion(f32[512,4096]{1,0:T(8,128)S(1)} %fusion.10, f32[512,4096]{1,0:T(8,128)S(1)} %fusion.6, bf16[1,512,4096]{2,1,0:T(8,128)(2,1)} %collective-permute-done.2, f32[1,512,512]{1,2,0:T(8,128)S(1)} %copy.11, f32[512,512]{1,0:T(8,128)S(1)} %fusion.32, pred[]{:T(512)} %bitcast.19), kind=kOutput, calls=%fused_computation | convolution fusion | flops 2152464384 | bytes 31457280 | tf_op jit(solution)/shard_map/rab,rbp->rap/dot_general | solution.py:44
Async XLA Ops:
  0.0 22.0 %copy-start.3 = (f32[512]{0:T(512)S(1)}, f32[512]{0:T(512)}, u32[]{:S(2)}) copy-start(f32[512]{0:T(512)} %param.6) | copy-start | bytes 6148
  0.0 22.0 %collective-permute-start.1 = (bf16[1,512,4096]{2,1,0:T(8,128)(2,1)}, bf16[1,512,4096]{2,1,0:T(8,128)(2,1)}, u32[]{:S(2)}, u32[]{:S(2)}) collective-permute-start(bf16[1,512,4096]{2,1,0:T(8,128)(2,1)} %param.4), channel_id=1, source_target_pairs={{0,1},{1,2},{2,3},{3,4},{4,5},{5,6},{6,7},{7,8},{8,9},{9,10},{10,1... | collective-permute-start | bytes 12582920 | tf_op jit(solution)/shard_map/ppermute | solution.py:15
  4.5 24.7 %collective-permute-start = (bf16[1,512,4096]{2,1,0:T(8,128)(2,1)}, bf16[1,512,4096]{2,1,0:T(8,128)(2,1)}, u32[]{:S(2)}, u32[]{:S(2)}) collective-permute-start(bf16[1,512,4096]{2,1,0:T(8,128)(2,1)} %param.4), channel_id=1, source_target_pairs={{1,0},{2,1},{3,2},{4,3},{5,4},{6,5},{7,6},{8,7},{9,8},{10,9},{11,1... | collective-permute-start | bytes 12582920 | tf_op jit(solution)/shard_map/ppermute | solution.py:17
  5.8 229.9 %collective-permute-start.2 = (bf16[1,512,4096]{2,1,0:T(8,128)(2,1)}, bf16[1,512,4096]{2,1,0:T(8,128)(2,1)}, u32[]{:S(2)}, u32[]{:S(2)}) collective-permute-start(bf16[1,512,4096]{2,1,0:T(8,128)(2,1)} %param.4), channel_id=1, source_target_pairs={{0,8},{1,9},{2,10},{3,11},{4,12},{5,13},{6,14},{7,15},{8,0},{9,1},... | collective-permute-start | bytes 12582920 | tf_op jit(solution)/shard_map/ppermute | solution.py:26
  35.0 1.0 copy-start
  244.1 5.0 %copy-start.1 = (f32[512,512]{1,0:T(8,128)S(1)}, f32[512,512]{1,0:T(8,128)}, u32[]{:S(2)}) copy-start(f32[512,512]{1,0:T(8,128)} %copy-done) | copy-start | bytes 3145732
  244.2 5.0 %copy-start.2 = (f32[1,512,512]{1,2,0:T(8,128)S(1)}, f32[1,512,512]{1,2,0:T(8,128)}, u32[]{:S(2)}) copy-start(f32[1,512,512]{1,2,0:T(8,128)} %copy.6) | copy-start | bytes 3145732
where the time goes:
time: 263 us
  waiting for transfers between devices  198 us (75%)
  matrix products  36.2 us (14%)
  starting transfers between devices  10.7 us (4%)
  local copies, waits for them, and re-layouts  9.79 us (4%)
  between operations  5.87 us (2%)
    ppermute x1, waiting for transfers between devices, passed_along(): lax.ppermute(shard, axis, [(i, (i + by) % peers) for i in range(peers)])  198 us
    dot_general x3, matrix products, apply_left(): jnp.einsum('rab,rbp->rap', weights, blocks, preferred_element_type=jnp.fl...  18.7 us
    dot_general x3, matrix products, amplitudes(): jnp.einsum('rap,rbp->rab', home_block, partner_block, preferred_element_t...  17.5 us
  transfers between devices with their start and end apart: 3, of which 1 were waited for; matrix products, arithmetic and copies ran while one was open for 8% of the time, Pallas kernels for 0%

commit v1 on v0

v1 whole, which is shorter than its diff:
```python
import functools

import jax
import jax.numpy as jnp
from jax import lax
from jax.experimental import pallas as pl
from jax.experimental.pallas import tpu as pltpu
from jax.sharding import PartitionSpec as P

MESH = pl.DeviceIdType.MESH
CHUNKS = 16
LOWER, UPPER, ACROSS = 0, 1, 2


def gather_kernel(
    count, own_hbm, eps_vir, eps_occ, mask, landed, weights,
    own, total, level, own_sem, up_sem, down_sem, far_sem, relay_sem, recv_sem,
):
    me = lax.axis_index("occ")
    half = count // 2
    width = own.shape[2]
    size = own.shape[1]
    last = count - 1
    partner = lax.rem(me + half, count)
    sends_up = (me < last) & (me != half - 1)
    sends_down = (me > 0) & (me != half)
    relays = (me == 0) | (me == last)
    late = (me == half - 1) | (me == half)
    relay_to = jnp.where(me == 0, half - 1, half)
    relay_slot = jnp.where(me == 0, UPPER, LOWER)
    relay_peer = jnp.where(me == half - 1, 0, jnp.where(me == half, last, relay_to))
    late_slot = jnp.where(me == half - 1, UPPER, LOWER)
    one = lambda flag: jnp.where(flag, 1, 0)

    def signal(to):
        pl.semaphore_signal(
            pltpu.get_barrier_semaphore(), inc=1, device_id={"occ": to}, device_id_type=MESH
        )

    signal(partner)
    pl.when(sends_up)(lambda: signal(me + 1))
    pl.when(sends_down)(lambda: signal(me - 1))
    pl.when(relays | late)(lambda: signal(relay_peer))
    pl.semaphore_wait(
        pltpu.get_barrier_semaphore(), 1 + one(sends_up) + one(sends_down) + one(relays | late)
    )

    def remote(source, k, slot, send_sem, to):
        return pltpu.make_async_remote_copy(
            src_ref=source, dst_ref=landed.at[k, slot], send_sem=send_sem.at[k],
            recv_sem=recv_sem.at[slot, k], device_id={"occ": to}, device_id_type=MESH,
        )

    def columns(k):
        return own_hbm.at[:, pl.ds(pl.multiple_of(k * width, width), width)]

    def up(k):
        return remote(columns(k), k, LOWER, up_sem, me + 1)

    def down(k):
        return remote(columns(k), k, UPPER, down_sem, me - 1)

    def far(k):
        return remote(columns(k), k, ACROSS, far_sem, partner)

    def relay(k):
        return remote(landed.at[k, ACROSS], k, relay_slot, relay_sem, relay_to)

    def loaded(k):
        return pltpu.make_async_copy(columns(k), own.at[k], own_sem.at[k])

    def received(k, slot):
        remote(landed.at[k, slot], k, slot, far_sem, partner).wait_recv()

    @pl.loop(0, CHUNKS)
    def _(k):
        pl.when(sends_up)(lambda: up(k).start())
        pl.when(sends_down)(lambda: down(k).start())

    @pl.loop(0, CHUNKS)
    def _(k):
        far(k).start()

    @pl.loop(0, CHUNKS)
    def _(k):
        loaded(k).start()

    rows = jnp.broadcast_to(eps_vir[...], (size, size))
    level[...] = rows + rows.T
    total[...] = jnp.zeros_like(total)

    @pl.when(me == 0)
    def _():
        landed[:, LOWER] = jnp.zeros((CHUNKS, size, width), landed.dtype)

    @pl.when(me == last)
    def _():
        landed[:, UPPER] = jnp.zeros((CHUNKS, size, width), landed.dtype)

    def accumulate(k, slot):
        received(k, slot)
        total[slot] += lax.dot_general(
            own[k], landed[k, slot], (((1,), (1,)), ((), ())), preferred_element_type=jnp.float32
        )

    def finish(slot):
        lower, upper = jnp.maximum(me - 1, 0), jnp.minimum(me + 1, last)
        other = (lower, upper, partner)[slot]
        bit = (mask[0, lower], mask[0, me], mask[1, jnp.minimum(me, partner)])[slot]
        real = (me > 0, me < last, me >= 0)[slot]
        keep = jnp.where(bit == 1, 1.0, 0.0) * jnp.where(real, 1.0, 0.0)
        single = -total[slot] / (level[...] - (eps_occ[me] + eps_occ[other]))
        doubled = (2.0 * single - single.T) * keep
        weights[:, slot * size : (slot + 1) * size] = doubled.astype(weights.dtype)

    lower_early = (me > 0) & (me != half)
    upper_early = (me < last) & (me != half - 1)

    @pl.loop(0, CHUNKS)
    def _(k):
        loaded(k).wait()
        pl.when(lower_early)(lambda: accumulate(k, LOWER))
        pl.when(upper_early)(lambda: accumulate(k, UPPER))

    pl.when(me != half)(lambda: finish(LOWER))
    pl.when(me != half - 1)(lambda: finish(UPPER))

    @pl.loop(0, CHUNKS)
    def _(k):
        received(k, ACROSS)
        pl.when(relays)(lambda: relay(k).start())
        total[ACROSS] += lax.dot_general(
            own[k], landed[k, ACROSS], (((1,), (1,)), ((), ())), preferred_element_type=jnp.float32
        )
        pl.when(late)(lambda: accumulate(k, late_slot))

    finish(ACROSS)
    pl.when(me == half)(lambda: finish(LOWER))
    pl.when(me == half - 1)(lambda: finish(UPPER))

    @pl.loop(0, CHUNKS)
    def _(k):
        pl.when(sends_up)(lambda: up(k).wait_send())
        pl.when(sends_down)(lambda: down(k).wait_send())
        far(k).wait_send()
        pl.when(relays)(lambda: relay(k).wait_send())


def apply_kernel(landed, weights, out, staged, sems):
    size, width = staged.shape[1:]

    def stored(k):
        slot = lax.rem(k, 2)
        at = pl.ds(pl.multiple_of(k * width, width), width)
        return pltpu.make_async_copy(staged.at[slot], out.at[:, at], sems.at[slot])

    @pl.loop(0, CHUNKS)
    def _(k):
        pl.when(k >= 2)(lambda: stored(k - 2).wait())
        blocks = landed[k].reshape(3 * size, width)
        staged[lax.rem(k, 2)] = jnp.dot(weights[...], blocks, preferred_element_type=jnp.float32)
        stored(k).start()

    stored(CHUNKS - 2).wait()
    stored(CHUNKS - 1).wait()


def local(orbital_blocks, eps_occ, eps_vir, pair_mask):
    _, size, aux = orbital_blocks.shape
    width = aux // CHUNKS
    count = lax.axis_size("occ")
    vmem = pl.BlockSpec(memory_space=pltpu.VMEM)
    smem = pl.BlockSpec(memory_space=pltpu.SMEM)
    hbm = pl.BlockSpec(memory_space=pl.ANY)
    per_chunk = pltpu.SemaphoreType.DMA((CHUNKS,))
    landed, weights = pl.pallas_call(
        functools.partial(gather_kernel, count),
        out_shape=(
            pltpu.VMEM((CHUNKS, 3, size, width), jnp.bfloat16),
            pltpu.VMEM((size, 3 * size), jnp.bfloat16),
        ),
        in_specs=[hbm, vmem, smem, smem],
        out_specs=(vmem, vmem),
        scratch_shapes=[
            pltpu.VMEM((CHUNKS, size, width), jnp.bfloat16),
            pltpu.VMEM((3, size, size), jnp.float32),
            pltpu.VMEM((size, size), jnp.float32),
            per_chunk, per_chunk, per_chunk, per_chunk, per_chunk,
            pltpu.SemaphoreType.DMA((3, CHUNKS)),
        ],
        compiler_params=pltpu.CompilerParams(
            collective_id=0, has_side_effects=True, vmem_limit_bytes=44 * 2**20
        ),
    )(orbital_blocks[0], eps_vir[None], eps_occ, pair_mask.T)
    gradient = pl.pallas_call(
        apply_kernel,
        out_shape=jax.ShapeDtypeStruct((size, aux), jnp.float32),
        in_specs=[vmem, vmem],
        out_specs=hbm,
        scratch_shapes=[
            pltpu.VMEM((2, size, width), jnp.float32),
            pltpu.SemaphoreType.DMA((2,)),
        ],
        compiler_params=pltpu.CompilerParams(vmem_limit_bytes=44 * 2**20),
    )(
        pltpu.with_memory_space_constraint(landed, pltpu.VMEM),
        pltpu.with_memory_space_constraint(weights, pltpu.VMEM),
    )
    return gradient[None]


def solution(mesh):
    in_specs = (P(("grp", "occ"), None, None), P("grp"), P("grp"), P("grp", None))
    out_specs = P(("grp", "occ"), None, None)
    return jax.shard_map(local, mesh=mesh, in_specs=in_specs, out_specs=out_specs, check_vma=False)
```

time: 263 us -> 205 us (0.78)
  the two profiles are of different devices: /device:TPU:0 before, /device:TPU:15 now
where the time goes in v1:
time: 205 us
  Pallas kernels  205 us (100%)
    pallas_call x1, Pallas kernels, local(): pl.pallas_call(functools.partial(gather_kernel, count), out_shape=(pltpu....  193 us
    pallas_call x1, Pallas kernels, local(): pl.pallas_call(apply_kernel, out_shape=jax.ShapeDtypeStruct((size, aux),...  11.5 us

profile of v1, /device:TPU:15, one launch (start us, length us, event | category | flops | bytes accessed | tf_op | source)
XLA Modules:
  0.0 204.7 jit_solution(2950383802146303706)
XLA Ops:
  0.0 193.1 %shard_map.46 = (bf16[16,3,512,256]{3,2,1,0:T(8,128)(2,1)S(1)}, bf16[512,1536]{1,0:T(8,128)(2,1)S(1)}) custom-call(bf16[512,4096]{1,0:T(8,128)(2,1)} %bitcast.4, f32[1,512]{1,0:T(1,128)} %bitcast.5, f32[16]{0:T(128)} %eps_occ.1, s32[2,16]{1,0:T(2,128)} %bitcast.6), custom_call_target="tpu_custom_call" | custom-call | tf_op jit(solution)/shard_map/pallas_call | solution.py:176
  193.2 11.5 %shard_map.47 = f32[512,4096]{1,0:T(8,128)} custom-call(bf16[16,3,512,256]{3,2,1,0:T(8,128)(2,1)S(1)} %get-tuple-element.7.landed, bf16[512,1536]{1,0:T(8,128)(2,1)S(1)} %get-tuple-element.8.weights), custom_call_target="tpu_custom_call" | custom-call | tf_op jit(solution)/shard_map/pallas_call | solution.py:195

commit v2 on v1

v2 whole, which is shorter than its diff:
```python
import functools

import jax
import jax.numpy as jnp
from jax import lax
from jax.experimental import pallas as pl
from jax.experimental.pallas import tpu as pltpu
from jax.sharding import PartitionSpec as P

MESH = pl.DeviceIdType.MESH
CHUNKS = 16
LOWER, UPPER, ACROSS = 0, 1, 2


def gather_kernel(
    count, own_hbm, eps_vir, eps_occ, mask, across, weights, gradient,
    near, near_weights, own, total, level,
    own_sem, up_sem, down_sem, far_sem, relay_sem, near_recv, across_recv,
):
    me = lax.axis_index("occ")
    half = count // 2
    size, width = own.shape[1:]
    last = count - 1
    partner = lax.rem(me + half, count)
    sends_up = (me < last) & (me != half - 1)
    sends_down = (me > 0) & (me != half)
    relays = (me == 0) | (me == last)
    relayed = (me == half - 1) | (me == half)
    yields = (me == half + 1) | (me == half - 2)
    relay_to = jnp.where(me == 0, half - 1, half)
    relay_slot = jnp.where(me == 0, UPPER, LOWER)
    relay_peer = jnp.where(me == half - 1, 0, jnp.where(me == half, last, relay_to))
    one = lambda flag: jnp.where(flag, 1, 0)

    def signal(to):
        pl.semaphore_signal(
            pltpu.get_barrier_semaphore(), inc=1, device_id={"occ": to}, device_id_type=MESH
        )

    signal(partner)
    pl.when(sends_up)(lambda: signal(me + 1))
    pl.when(sends_down)(lambda: signal(me - 1))
    pl.when(relays | relayed)(lambda: signal(relay_peer))
    pl.semaphore_wait(
        pltpu.get_barrier_semaphore(), 1 + one(sends_up) + one(sends_down) + one(relays | relayed)
    )

    def columns(k):
        return own_hbm.at[:, pl.ds(pl.multiple_of(k * width, width), width)]

    def to_near(source, k, slot, send_sem, to):
        return pltpu.make_async_remote_copy(
            src_ref=source, dst_ref=near.at[k, slot], send_sem=send_sem.at[k],
            recv_sem=near_recv.at[slot, k], device_id={"occ": to}, device_id_type=MESH,
        )

    def up(k):
        return to_near(columns(k), k, LOWER, up_sem, me + 1)

    def down(k):
        return to_near(columns(k), k, UPPER, down_sem, me - 1)

    def relay(k):
        return to_near(across.at[k], k, relay_slot, relay_sem, relay_to)

    def far(k):
        return pltpu.make_async_remote_copy(
            src_ref=columns(k), dst_ref=across.at[k], send_sem=far_sem.at[k],
            recv_sem=across_recv.at[k], device_id={"occ": partner}, device_id_type=MESH,
        )

    def loaded(k):
        return pltpu.make_async_copy(columns(k), own.at[k], own_sem.at[k])

    def send_far():
        @pl.loop(0, CHUNKS)
        def _(k):
            far(k).start()

    @pl.loop(0, CHUNKS)
    def _(k):
        pl.when(sends_up)(lambda: up(k).start())
        pl.when(sends_down)(lambda: down(k).start())

    pl.when(jnp.logical_not(yields))(send_far)

    @pl.loop(0, CHUNKS)
    def _(k):
        loaded(k).start()

    rows = jnp.broadcast_to(eps_vir[...], (size, size))
    level[...] = rows + rows.T
    total[...] = jnp.zeros_like(total)

    @pl.when(me == 0)
    def _():
        near[:, LOWER] = jnp.zeros((CHUNKS, size, width), near.dtype)

    @pl.when(me == last)
    def _():
        near[:, UPPER] = jnp.zeros((CHUNKS, size, width), near.dtype)

    def overlap(k, block):
        return lax.dot_general(
            own[k], block, (((1,), (1,)), ((), ())), preferred_element_type=jnp.float32
        )

    def accumulate(k, slot):
        to_near(near.at[k, slot], k, slot, far_sem, partner).wait_recv()
        total[slot] += overlap(k, near[k, slot])

    def kept(bit, real):
        return jnp.where(bit == 1, 1.0, 0.0) * jnp.where(real, 1.0, 0.0)

    def finish(slot, keep, other):
        single = -total[slot] / (level[...] - (eps_occ[me] + eps_occ[other]))
        doubled = (2.0 * single - single.T) * keep
        near_weights[:, slot * size : (slot + 1) * size] = doubled.astype(near_weights.dtype)

    @pl.loop(0, CHUNKS)
    def _(k):
        loaded(k).wait()
        pl.when(me > 0)(lambda: accumulate(k, LOWER))
        pl.when(me < last)(lambda: accumulate(k, UPPER))

    pl.when(yields)(send_far)
    lower, upper = jnp.maximum(me - 1, 0), jnp.minimum(me + 1, last)
    finish(LOWER, kept(mask[0, lower], me > 0), lower)
    finish(UPPER, kept(mask[0, me], me < last), upper)
    level[...] = kept(mask[1, jnp.minimum(me, partner)], me >= 0) / (
        level[...] - (eps_occ[me] + eps_occ[partner])
    )

    @pl.loop(0, CHUNKS)
    def _(k):
        gradient[k] = jnp.dot(
            near_weights[...], near[k].reshape(2 * size, width), preferred_element_type=jnp.float32
        )

    @pl.loop(0, CHUNKS)
    def _(k):
        far(k).wait_recv()
        pl.when(relays)(lambda: relay(k).start())
        total[ACROSS] += overlap(k, across[k])

    single = -total[ACROSS] * level[...]
    weights[...] = (2.0 * single - single.T).astype(weights.dtype)

    @pl.loop(0, CHUNKS)
    def _(k):
        pl.when(sends_up)(lambda: up(k).wait_send())
        pl.when(sends_down)(lambda: down(k).wait_send())
        far(k).wait_send()
        pl.when(relays)(lambda: relay(k).wait_send())


def apply_kernel(across, weights, gradient, out, staged, sems):
    size, width = staged.shape[1:]

    def stored(k):
        slot = lax.rem(k, 2)
        at = pl.ds(pl.multiple_of(k * width, width), width)
        return pltpu.make_async_copy(staged.at[slot], out.at[:, at], sems.at[slot])

    @pl.loop(0, CHUNKS)
    def _(k):
        pl.when(k >= 2)(lambda: stored(k - 2).wait())
        staged[lax.rem(k, 2)] = gradient[k] + jnp.dot(
            weights[...], across[k], preferred_element_type=jnp.float32
        )
        stored(k).start()

    stored(CHUNKS - 2).wait()
    stored(CHUNKS - 1).wait()


def local(orbital_blocks, eps_occ, eps_vir, pair_mask):
    _, size, aux = orbital_blocks.shape
    width = aux // CHUNKS
    count = lax.axis_size("occ")
    vmem = pl.BlockSpec(memory_space=pltpu.VMEM)
    smem = pl.BlockSpec(memory_space=pltpu.SMEM)
    hbm = pl.BlockSpec(memory_space=pl.ANY)
    per_chunk = pltpu.SemaphoreType.DMA((CHUNKS,))
    arrived = pl.pallas_call(
        functools.partial(gather_kernel, count),
        out_shape=(
            pltpu.VMEM((CHUNKS, size, width), jnp.bfloat16),
            pltpu.VMEM((size, size), jnp.bfloat16),
            pltpu.VMEM((CHUNKS, size, width), jnp.float32),
        ),
        in_specs=[hbm, vmem, smem, smem],
        out_specs=(vmem, vmem, vmem),
        scratch_shapes=[
            pltpu.VMEM((CHUNKS, 2, size, width), jnp.bfloat16),
            pltpu.VMEM((size, 2 * size), jnp.bfloat16),
            pltpu.VMEM((CHUNKS, size, width), jnp.bfloat16),
            pltpu.VMEM((3, size, size), jnp.float32),
            pltpu.VMEM((size, size), jnp.float32),
            per_chunk, per_chunk, per_chunk, per_chunk, per_chunk,
            pltpu.SemaphoreType.DMA((2, CHUNKS)),
            per_chunk,
        ],
        compiler_params=pltpu.CompilerParams(
            collective_id=0, has_side_effects=True, vmem_limit_bytes=44 * 2**20
        ),
    )(orbital_blocks[0], eps_vir[None], eps_occ, pair_mask.T)
    gradient = pl.pallas_call(
        apply_kernel,
        out_shape=jax.ShapeDtypeStruct((size, aux), jnp.float32),
        in_specs=[vmem, vmem, vmem],
        out_specs=hbm,
        scratch_shapes=[
            pltpu.VMEM((2, size, width), jnp.float32),
            pltpu.SemaphoreType.DMA((2,)),
        ],
        compiler_params=pltpu.CompilerParams(vmem_limit_bytes=44 * 2**20),
    )(*(pltpu.with_memory_space_constraint(array, pltpu.VMEM) for array in arrived))
    return gradient[None]


def solution(mesh):
    in_specs = (P(("grp", "occ"), None, None), P("grp"), P("grp"), P("grp", None))
    out_specs = P(("grp", "occ"), None, None)
    return jax.shard_map(local, mesh=mesh, in_specs=in_specs, out_specs=out_specs, check_vma=False)
```

time: 205 us -> 199 us (0.971)
  the two profiles are of different devices: /device:TPU:15 before, /device:TPU:1 now
where the time goes in v2:
time: 199 us
  Pallas kernels  199 us (100%)
    pallas_call x1, Pallas kernels, local(): pl.pallas_call(functools.partial(gather_kernel, count), out_shape=(pltpu....  190 us
    pallas_call x1, Pallas kernels, local(): pl.pallas_call(apply_kernel, out_shape=jax.ShapeDtypeStruct((size, aux),...  9.03 us

profile of v2, /device:TPU:1, one launch (start us, length us, event | category | flops | bytes accessed | tf_op | source)
XLA Modules:
  0.0 198.7 jit_solution(15479043178841498503)
XLA Ops:
  0.0 189.7 %shard_map.46 = (bf16[16,512,256]{2,1,0:T(8,128)(2,1)S(1)}, bf16[512,512]{1,0:T(8,128)(2,1)S(1)}, f32[16,512,256]{2,1,0:T(8,128)S(1)}) custom-call(bf16[512,4096]{1,0:T(8,128)(2,1)} %bitcast.4, f32[1,512]{1,0:T(1,128)} %bitcast.5, f32[16]{0:T(128)} %eps_occ.1, s32[2,16]{1,0:T(2,128)} %bitcast.6), custom_call_target="tpu_custom_call" | custom-call | tf_op jit(solution)/shard_map/pallas_call | solution.py:185
  189.7 9.0 %shard_map.47 = f32[512,4096]{1,0:T(8,128)} custom-call(bf16[16,512,256]{2,1,0:T(8,128)(2,1)S(1)} %get-tuple-element.8.across, bf16[512,512]{1,0:T(8,128)(2,1)S(1)} %get-tuple-element.9.weights, f32[16,512,256]{2,1,0:T(8,128)S(1)} %get-tuple-element.10.gradient), custom_call_target="tpu_custom_call" | custom-call | tf_op jit(solution)/shard_map/pallas_call | solution.py:208

commit v3 on v2

--- a/solution.py
+++ b/solution.py
@@ -8,7 +8,7 @@
 from jax.sharding import PartitionSpec as P
 
 MESH = pl.DeviceIdType.MESH
-CHUNKS = 16
+CHUNKS = 8
 LOWER, UPPER, ACROSS = 0, 1, 2
 
 
@@ -72,17 +72,19 @@
     def loaded(k):
         return pltpu.make_async_copy(columns(k), own.at[k], own_sem.at[k])
 
-    def send_far():
-        @pl.loop(0, CHUNKS)
+    def send_far(first):
+        @pl.loop(first, CHUNKS)
         def _(k):
             far(k).start()
 
+    pl.when(jnp.logical_not(yields))(lambda: far(0).start())
+
     @pl.loop(0, CHUNKS)
     def _(k):
         pl.when(sends_up)(lambda: up(k).start())
         pl.when(sends_down)(lambda: down(k).start())
 
-    pl.when(jnp.logical_not(yields))(send_far)
+    pl.when(jnp.logical_not(yields))(lambda: send_far(1))
 
     @pl.loop(0, CHUNKS)
     def _(k):
@@ -123,7 +125,7 @@
         pl.when(me > 0)(lambda: accumulate(k, LOWER))
         pl.when(me < last)(lambda: accumulate(k, UPPER))
 
-    pl.when(yields)(send_far)
+    pl.when(yields)(lambda: send_far(0))
     lower, upper = jnp.maximum(me - 1, 0), jnp.minimum(me + 1, last)
     finish(LOWER, kept(mask[0, lower], me > 0), lower)
     finish(UPPER, kept(mask[0, me], me < last), upper)
@@ -139,6 +141,11 @@
 
     @pl.loop(0, CHUNKS)
     def _(k):
+        pl.when(sends_up)(lambda: up(k).wait_send())
+        pl.when(sends_down)(lambda: down(k).wait_send())
+
+    @pl.loop(0, CHUNKS)
+    def _(k):
         far(k).wait_recv()
         pl.when(relays)(lambda: relay(k).start())
         total[ACROSS] += overlap(k, across[k])
@@ -148,30 +155,27 @@
 
     @pl.loop(0, CHUNKS)
     def _(k):
-        pl.when(sends_up)(lambda: up(k).wait_send())
-        pl.when(sends_down)(lambda: down(k).wait_send())
         far(k).wait_send()
         pl.when(relays)(lambda: relay(k).wait_send())
 
 
 def apply_kernel(across, weights, gradient, out, staged, sems):
-    size, width = staged.shape[1:]
+    width = staged.shape[2]
 
     def stored(k):
-        slot = lax.rem(k, 2)
         at = pl.ds(pl.multiple_of(k * width, width), width)
-        return pltpu.make_async_copy(staged.at[slot], out.at[:, at], sems.at[slot])
-
-    @pl.loop(0, CHUNKS)
-    def _(k):
-        pl.when(k >= 2)(lambda: stored(k - 2).wait())
-        staged[lax.rem(k, 2)] = gradient[k] + jnp.dot(
+        return pltpu.make_async_copy(staged.at[k], out.at[:, at], sems.at[k])
+
+    @pl.loop(0, CHUNKS)
+    def _(k):
+        staged[k] = gradient[k] + jnp.dot(
             weights[...], across[k], preferred_element_type=jnp.float32
         )
         stored(k).start()
 
-    stored(CHUNKS - 2).wait()
-    stored(CHUNKS - 1).wait()
+    @pl.loop(0, CHUNKS)
+    def _(k):
+        stored(k).wait()
 
 
 def local(orbital_blocks, eps_occ, eps_vir, pair_mask):
@@ -211,8 +215,8 @@
         in_specs=[vmem, vmem, vmem],
         out_specs=hbm,
         scratch_shapes=[
-            pltpu.VMEM((2, size, width), jnp.float32),
-            pltpu.SemaphoreType.DMA((2,)),
+            pltpu.VMEM((CHUNKS, size, width), jnp.float32),
+            per_chunk,
         ],
         compiler_params=pltpu.CompilerParams(vmem_limit_bytes=44 * 2**20),
     )(*(pltpu.with_memory_space_constraint(array, pltpu.VMEM) for array in arrived))

time: 199 us -> 194 us (0.975)
  Pallas kernels: 199 us -> 194 us
    pallas_call x1, Pallas kernels: 9.03 us -> 4.56 us  [local(): pl.pallas_call(apply_kernel, out_shape=jax.ShapeDtypeStruct((size, aux),...]
where the time goes in v3:
time: 194 us
  Pallas kernels  194 us (100%)
    pallas_call x1, Pallas kernels, local(): pl.pallas_call(functools.partial(gather_kernel, count), out_shape=(pltpu....  189 us
    pallas_call x1, Pallas kernels, local(): pl.pallas_call(apply_kernel, out_shape=jax.ShapeDtypeStruct((size, aux),...  4.56 us

profile of v3, /device:TPU:1, one launch (start us, length us, event | category | flops | bytes accessed | tf_op | source)
XLA Modules:
  0.0 193.6 jit_solution(15947358902557307590)
XLA Ops:
  0.0 189.0 %shard_map.46 = (bf16[8,512,512]{2,1,0:T(8,128)(2,1)S(1)}, bf16[512,512]{1,0:T(8,128)(2,1)S(1)}, f32[8,512,512]{2,1,0:T(8,128)S(1)}) custom-call(bf16[512,4096]{1,0:T(8,128)(2,1)} %bitcast.4, f32[1,512]{1,0:T(1,128)} %bitcast.5, f32[16]{0:T(128)} %eps_occ.1, s32[2,16]{1,0:T(2,128)} %bitcast.6), custom_call_target="tpu_custom_call" | custom-call | tf_op jit(solution)/shard_map/pallas_call | solution.py:189
  189.0 4.6 %shard_map.47 = f32[512,4096]{1,0:T(8,128)} custom-call(bf16[8,512,512]{2,1,0:T(8,128)(2,1)S(1)} %get-tuple-element.8.across, bf16[512,512]{1,0:T(8,128)(2,1)S(1)} %get-tuple-element.9.weights, f32[8,512,512]{2,1,0:T(8,128)S(1)} %get-tuple-element.10.gradient), custom_call_target="tpu_custom_call" | custom-call | tf_op jit(solution)/shard_map/pallas_call | solution.py:212

commit v4 on v3

--- a/solution.py
+++ b/solution.py
@@ -94,13 +94,7 @@
     level[...] = rows + rows.T
     total[...] = jnp.zeros_like(total)
 
-    @pl.when(me == 0)
-    def _():
-        near[:, LOWER] = jnp.zeros((CHUNKS, size, width), near.dtype)
-
-    @pl.when(me == last)
-    def _():
-        near[:, UPPER] = jnp.zeros((CHUNKS, size, width), near.dtype)
+    gradient[...] = jnp.zeros_like(gradient)
 
     def overlap(k, block):
         return lax.dot_general(
@@ -111,33 +105,35 @@
         to_near(near.at[k, slot], k, slot, far_sem, partner).wait_recv()
         total[slot] += overlap(k, near[k, slot])
 
-    def kept(bit, real):
-        return jnp.where(bit == 1, 1.0, 0.0) * jnp.where(real, 1.0, 0.0)
-
-    def finish(slot, keep, other):
-        single = -total[slot] / (level[...] - (eps_occ[me] + eps_occ[other]))
-        doubled = (2.0 * single - single.T) * keep
-        near_weights[:, slot * size : (slot + 1) * size] = doubled.astype(near_weights.dtype)
-
-    @pl.loop(0, CHUNKS)
-    def _(k):
-        loaded(k).wait()
-        pl.when(me > 0)(lambda: accumulate(k, LOWER))
-        pl.when(me < last)(lambda: accumulate(k, UPPER))
+    def kept(bit):
+        return jnp.where(bit == 1, 1.0, 0.0)
+
+    @pl.loop(0, 2)
+    def _(turn):
+        slot = jnp.where(me == half, 1 - turn, turn)
+        other = jnp.where(slot == LOWER, me - 1, me + 1)
+
+        @pl.loop(0, CHUNKS)
+        def _(k):
+            pl.when(turn == 0)(lambda: loaded(k).wait())
+            pl.when((other >= 0) & (other < count))(lambda: accumulate(k, slot))
+
+        @pl.when((other >= 0) & (other < count))
+        def _():
+            single = -total[slot] / (level[...] - (eps_occ[me] + eps_occ[other]))
+            doubled = (2.0 * single - single.T) * kept(mask[0, jnp.minimum(me, other)])
+            near_weights[...] = doubled.astype(near_weights.dtype)
+
+            @pl.loop(0, CHUNKS)
+            def _(k):
+                gradient[k] += jnp.dot(
+                    near_weights[...], near[k, slot], preferred_element_type=jnp.float32
+                )
 
     pl.when(yields)(lambda: send_far(0))
-    lower, upper = jnp.maximum(me - 1, 0), jnp.minimum(me + 1, last)
-    finish(LOWER, kept(mask[0, lower], me > 0), lower)
-    finish(UPPER, kept(mask[0, me], me < last), upper)
-    level[...] = kept(mask[1, jnp.minimum(me, partner)], me >= 0) / (
+    level[...] = kept(mask[1, jnp.minimum(me, partner)]) / (
         level[...] - (eps_occ[me] + eps_occ[partner])
     )
-
-    @pl.loop(0, CHUNKS)
-    def _(k):
-        gradient[k] = jnp.dot(
-            near_weights[...], near[k].reshape(2 * size, width), preferred_element_type=jnp.float32
-        )
 
     @pl.loop(0, CHUNKS)
     def _(k):
@@ -197,7 +193,7 @@
         out_specs=(vmem, vmem, vmem),
         scratch_shapes=[
             pltpu.VMEM((CHUNKS, 2, size, width), jnp.bfloat16),
-            pltpu.VMEM((size, 2 * size), jnp.bfloat16),
+            pltpu.VMEM((size, size), jnp.bfloat16),
             pltpu.VMEM((CHUNKS, size, width), jnp.bfloat16),
             pltpu.VMEM((3, size, size), jnp.float32),
             pltpu.VMEM((size, size), jnp.float32),

time: 194 us -> 194 us (level)
  no operation moved by 1% of the time
where the time goes in v4:
time: 194 us
  Pallas kernels  194 us (100%)
    pallas_call x1, Pallas kernels, local(): pl.pallas_call(functools.partial(gather_kernel, count), out_shape=(pltpu....  189 us
    pallas_call x1, Pallas kernels, local(): pl.pallas_call(apply_kernel, out_shape=jax.ShapeDtypeStruct((size, aux),...  4.56 us

profile of v4, /device:TPU:1, one launch (start us, length us, event | category | flops | bytes accessed | tf_op | source)
XLA Modules:
  0.0 193.6 jit_solution(3366138515734191864)
XLA Ops:
  0.0 189.0 %shard_map.46 = (bf16[8,512,512]{2,1,0:T(8,128)(2,1)S(1)}, bf16[512,512]{1,0:T(8,128)(2,1)S(1)}, f32[8,512,512]{2,1,0:T(8,128)S(1)}) custom-call(bf16[512,4096]{1,0:T(8,128)(2,1)} %bitcast.4, f32[1,512]{1,0:T(1,128)} %bitcast.5, f32[16]{0:T(128)} %eps_occ.1, s32[2,16]{1,0:T(2,128)} %bitcast.6), custom_call_target="tpu_custom_call" | custom-call | tf_op jit(solution)/shard_map/pallas_call | solution.py:185
  189.0 4.6 %shard_map.47 = f32[512,4096]{1,0:T(8,128)} custom-call(bf16[8,512,512]{2,1,0:T(8,128)(2,1)S(1)} %get-tuple-element.8.across, bf16[512,512]{1,0:T(8,128)(2,1)S(1)} %get-tuple-element.9.weights, f32[8,512,512]{2,1,0:T(8,128)S(1)} %get-tuple-element.10.gradient), custom_call_target="tpu_custom_call" | custom-call | tf_op jit(solution)/shard_map/pallas_call | solution.py:208
